TPU v7x, 32 devices: a whole 2x2x4 slice. The times are simulated.
32 devices in a mesh: frames: 8 (over y, x, core), pix: 4 (over z).
Axes of the slice: x: 2, y: 2, z: 4, core: 2. Of those that a mesh axis runs over, the one named last changes fastest.
Arguments:
- edge_frames: int32 [2, 1536], P(None, 'frames'), may hold values from 0 to 127, as said below
- rotvec: float32 [3, 128], replicated, may hold values from -0.06 to 0.06
- trans: float32 [3, 128], replicated, may hold values from -0.15 to 0.15
- inv_depth: float32 [128, 3072], P('frames', 'pix'), may hold values from 0.2 to 1
- depth_damping: float32 [128, 3072], P('frames', 'pix'), may hold values from 0.01 to 0.1
- flow: float32 [1536, 2, 3072], P('frames', None, 'pix'), may hold values from -0.3 to 0.3
- weight: float32 [1536, 2, 3072], P('frames', None, 'pix'), may hold values from 0.02 to 1
- mask: int32 [1536, 3072], P('frames', 'pix'), may hold values 0 or 1
Outputs:
- pose_step: float32 [6, 128], P(None, 'frames')
- depth_step: float32 [128, 3072], P('frames', 'pix')
Inputs may be any that keep to these rules, and one draw needn't show every extreme that they name: Edge e of the block of 192 edges held by one index of frames has its target edge_frames[1, e] among that index's 16 keyframes; its source edge_frames[0, e] differs from the target by 1 to 8, and in every block some source lies exactly 8 away.
All inputs are finite; a program needn't handle non-finite values. No bound on the sum of `mask` on one device may be relied on, other than what follows from the above.
Results may differ from a plain program's by a relative error of at most 0.00015.
Values sent between devices are 32-bit elements; how exact they have to be, the bound alone decides.
A program may use at most 64 MiB of HBM per device.

v0:
```python
import functools
import jax
import jax.numpy as jnp
from jax import lax
from jax.experimental import pallas as pl
from jax.experimental.pallas import tpu as pltpu
from jax.sharding import PartitionSpec as P

ROWS = 48
COLS = 64
RADIUS = 8
ITERS = 6
REG = 100.0
F32 = jnp.float32
BF16 = jnp.bfloat16
L = 128
WIN = 32
SLOT = 24
VMEM_LIMIT = 60 * 1024 * 1024
UPPER = [(i, j) for i in range(6) for j in range(i, 6) if (i, j) != (0, 1)]


def split(x):
    high = x.astype(BF16)
    return high, (x - high.astype(F32)).astype(BF16)


def iota(shape, dim):
    return lax.broadcasted_iota(jnp.int32, shape, dim)


def aggregate(dest_ref, flow_ref, weight_ref, mask_ref, own_ref, low_ref, high_ref):
    edges = dest_ref.shape[1]
    tiles = mask_ref.shape[1] // L
    own = own_ref.shape[1]
    side = low_ref.shape[1]
    rows = own + 2 * side
    pick = (iota((rows, edges), 0) == dest_ref[...]).astype(F32).astype(BF16)
    for tile in range(tiles):
        cols = slice(tile * L, (tile + 1) * L)
        live = mask_ref[:, cols].astype(F32)
        fields = []
        for comp in range(2):
            take = pl.ds(tile * 2 + comp, edges, stride=2 * tiles)
            conf = weight_ref[take, :] * live
            fields += [conf, conf * flow_ref[take, :]]
        high, low = split(jnp.concatenate(fields, axis=1))
        out = jnp.dot(pick, high, preferred_element_type=F32) + jnp.dot(
            pick, low, preferred_element_type=F32
        )
        for field in range(4):
            part = out[:, field * L : (field + 1) * L]
            own_ref[field, :, cols] = part[:own]
            low_ref[field, :, cols] = part[own : own + side]
            high_ref[field, :, cols] = part[own + side :]


def jac_sums(u, v, uu, vv, uv, ds, a, b):
    return [
        ds * a,
        ds * b,
        -ds * (u * a + v * b),
        -uv * a - vv * b,
        uu * a + uv * b,
        u * b - v * a,
    ]


def adj_t(rel, cor, vec):
    out = []
    for j in range(3):
        out.append(rel[j] * vec[0] + rel[3 + j] * vec[1] + rel[6 + j] * vec[2])
    for j in range(3):
        out.append(
            cor[j] * vec[0]
            + cor[3 + j] * vec[1]
            + cor[6 + j] * vec[2]
            + rel[j] * vec[3]
            + rel[3 + j] * vec[4]
            + rel[6 + j] * vec[5]
        )
    return out


def build(
    first_ref, pose_ref, own_ref, low_ref, high_ref, depth_ref, damp_ref,
    matrix_ref, zh_ref, zl_ref, base_ref, scale_ref,
    frame_ref, pair_ref, hacc, racc, hc, rc, adc, wide, depth3, damp3,
):
    f_dev, pix = depth_ref.shape
    tiles = pix // L
    half = f_dev // 2
    ox, oy, oz = pose_ref[0], pose_ref[1], pose_ref[2]
    zero = jnp.zeros_like(ox)
    cross = [[zero, -oz, oy], [oz, zero, -ox], [-oy, ox, zero]]
    sq = ox * ox + oy * oy + oz * oz
    c1 = 1.0 - sq / 6.0 + sq * sq / 120.0
    c2 = 0.5 - sq / 24.0 + sq * sq / 720.0
    for r in range(3):
        for c in range(3):
            square = cross[r][0] * cross[0][c] + cross[r][1] * cross[1][c] + cross[r][2] * cross[2][c]
            frame_ref[3 * r + c] = float(r == c) + c1 * cross[r][c] + c2 * square
        frame_ref[9 + r] = pose_ref[3 + r]
    for tile in range(tiles):
        depth3[tile] = depth_ref[:, tile * L : (tile + 1) * L]
        damp3[tile] = damp_ref[:, tile * L : (tile + 1) * L]
    hc[...] = jnp.zeros_like(hc)
    rc[...] = jnp.zeros_like(rc)
    adc[...] = jnp.zeros_like(adc)
    lane = iota((SLOT, L), 1)
    row = iota((SLOT, L), 0)
    row8 = iota((8, L), 0)

    for part in range(2):
        base = part * half
        win = slice(base, base + SLOT)
        if part == 0:
            pad = lambda x: jnp.concatenate([x, jnp.zeros((WIN - SLOT, L), F32)], axis=0)
        else:
            pad = lambda x: jnp.concatenate([jnp.zeros((WIN - SLOT, L), F32), x], axis=0)

        @pl.loop(0, half)
        def per_source(i):
            s = i + base
            here = [frame_ref[k, pl.ds(s + RADIUS, 1), :] for k in range(12)]
            there = [frame_ref[k, win, :] for k in range(12)]
            rel = [
                there[3 * r] * here[3 * c]
                + there[3 * r + 1] * here[3 * c + 1]
                + there[3 * r + 2] * here[3 * c + 2]
                for r in range(3)
                for c in range(3)
            ]
            tr = [
                there[9 + r]
                - (rel[3 * r] * here[9] + rel[3 * r + 1] * here[10] + rel[3 * r + 2] * here[11])
                for r in range(3)
            ]
            cor = []
            for c in range(3):
                cor.append(tr[1] * rel[6 + c] - tr[2] * rel[3 + c])
            for c in range(3):
                cor.append(tr[2] * rel[c] - tr[0] * rel[6 + c])
            for c in range(3):
                cor.append(tr[0] * rel[3 + c] - tr[1] * rel[c])
            at = lane == s + RADIUS
            for k in range(9):
                pair_ref[k] = rel[k]
                pair_ref[12 + k] = cor[k]
                adc[k, win, :] = jnp.where(at, rel[k], adc[k, win, :])
                adc[9 + k, win, :] = jnp.where(at, cor[k], adc[9 + k, win, :])
            for k in range(3):
                pair_ref[9 + k] = tr[k]
            hacc[...] = jnp.zeros_like(hacc)
            racc[...] = jnp.zeros_like(racc)
            if part == 0:
                slot = jnp.where(i == 0, 4, jnp.where(i <= 4, i - 1, 7 - i))
                shift = jnp.where(i > 4, i, 0)
                keep = row8 >= i
            else:
                slot = jnp.where(i <= 3, i, jnp.where(i == 7, 4, 6 - i))
                shift = jnp.where((i > 3) & (i < 7), i + 1, 0)
                keep = row8 <= i
            is_source = row == s + RADIUS - base

            def per_tile(tile):
                cols = slice(tile * L, (tile + 1) * L)
                fields = []
                for k in range(4):
                    src = high_ref if part == 0 else low_ref
                    got = src[k, pl.ds(pl.multiple_of(slot * 8, 8), 8), cols]
                    got = jnp.where(keep, pltpu.roll(got, shift, 0), 0.0)
                    if part == 0:
                        mine = own_ref[k, pl.ds(pl.multiple_of(s * SLOT + 8, 8), 16), cols]
                        fields.append(jnp.concatenate([got, mine], axis=0))
                    else:
                        mine = own_ref[k, pl.ds(pl.multiple_of(s * SLOT, 8), 16), cols]
                        fields.append(jnp.concatenate([mine, got], axis=0))
                wu, fu, wv, fv = fields
                pixel = first_ref[0] + tile * L + iota((1, L), 1)
                prow = pixel // COLS
                pcol = pixel - prow * COLS
                col = (pcol.astype(F32) - 0.5 * (COLS - 1)) / COLS
                rowc = (prow.astype(F32) - 0.5 * (ROWS - 1)) / COLS
                depth = depth3[tile, pl.ds(s, 1), :]
                m = [pair_ref[k] for k in range(21)]
                point = [
                    m[3 * k] * col + m[3 * k + 1] * rowc + m[3 * k + 2] + depth * m[9 + k]
                    for k in range(3)
                ]
                iz = 1.0 / point[2]
                u = point[0] * iz
                v = point[1] * iz
                ds = depth * iz
                su = iz * (m[9] - u * m[11])
                sv = iz * (m[10] - v * m[11])
                au = wu * su
                av = wv * sv
                gu = wu * (col - u) + fu
                gv = wv * (rowc - v) + fv
                curv = jnp.sum(au * su + av * sv, axis=0, keepdims=True) + damp3[tile, pl.ds(s, 1), :]
                grad = -jnp.sum(su * gu + sv * gv, axis=0, keepdims=True)
                bstep = grad / curv
                scale = 1.0 / jnp.sqrt(curv)
                base_ref[tile, pl.ds(s, 1), :] = bstep
                scale_ref[tile, pl.ds(s, 1), :] = scale
                uu = 1.0 + u * u
                vv = 1.0 + v * v
                uv = u * v
                e = jac_sums(u, v, uu, vv, uv, ds, au, av)
                back = adj_t(m[0:9], m[12:21], e)
                zcols = pl.ds(pl.multiple_of(s * pix + tile * L, L), L)
                for j in range(6):
                    total = -jnp.sum(back[j], axis=0, keepdims=True)
                    full = jnp.where(is_source, total, e[j]) * scale
                    high, low = split(pad(full))
                    zh_ref[j * WIN : (j + 1) * WIN, zcols] = high
                    zl_ref[j * WIN : (j + 1) * WIN, zcols] = low
                r = jac_sums(u, v, uu, vv, uv, ds, -gu - au * bstep, -gv - av * bstep)
                for j in range(6):
                    racc[j] += r[j]
                ju = [ds, None, -ds * u, -uv, uu, -v]
                jv = [None, ds, -ds * v, -vv, uv, u]
                wju = [None if x is None else wu * x for x in ju]
                wjv = [None if x is None else wv * x for x in jv]
                for n, (a, b) in enumerate(UPPER):
                    terms = []
                    if ju[a] is not None and ju[b] is not None:
                        terms.append(wju[a] * ju[b])
                    if jv[a] is not None and jv[b] is not None:
                        terms.append(wjv[a] * jv[b])
                    hacc[n] += terms[0] if len(terms) == 1 else terms[0] + terms[1]

            for tile in range(tiles):
                per_tile(tile)
            for n in range(len(UPPER)):
                hc[n, win, :] = jnp.where(at, jnp.sum(hacc[n], axis=1, keepdims=True), hc[n, win, :])
            for j in range(6):
                rc[j, win, :] = jnp.where(at, jnp.sum(racc[j], axis=1, keepdims=True), rc[j, win, :])

    def accumulate(s, carry):
        hh, hl = carry
        cols = pl.ds(pl.multiple_of(s * pix, L), pix)
        zh = zh_ref[:, cols]
        zl = zl_ref[:, cols]
        nt = (((1,), (1,)), ((), ()))
        return (
            hh + lax.dot_general(zh, zh, nt, preferred_element_type=F32),
            hl + lax.dot_general(zh, zl, nt, preferred_element_type=F32),
        )

    none = jnp.zeros((6 * WIN, 6 * WIN), F32)
    hh, hl = lax.fori_loop(0, f_dev, accumulate, (none, none))

    h = [[None] * 6 for _ in range(6)]
    for n, (a, b) in enumerate(UPPER):
        h[a][b] = hc[n]
        h[b][a] = h[a][b]
    rel = [adc[k] for k in range(9)]
    cor = [adc[9 + k] for k in range(9)]
    ad = [[None] * 6 for _ in range(6)]
    for i in range(3):
        for j in range(3):
            ad[i][j] = rel[3 * i + j]
            ad[i][3 + j] = cor[3 * i + j]
            ad[3 + i][3 + j] = rel[3 * i + j]
    lane = iota((WIN, L), 1)
    row = iota((WIN, L), 0)
    eye = row == lane

    def total(terms):
        out = None
        for x, y in terms:
            if x is None or y is None:
                continue
            out = x * y if out is None else out + x * y
        return out

    had = [[total([(h[i][k], ad[k][j]) for k in range(6)]) for j in range(6)] for i in range(6)]
    wide[...] = jnp.zeros_like(wide)
    matrix_ref[...] = jnp.zeros_like(matrix_ref)
    for i in range(6):
        rows = slice(i * WIN, (i + 1) * WIN)
        for j in range(6):
            cols = slice(j * WIN, (j + 1) * WIN)
            wide[rows, cols] = -had[i][j][:, :WIN]
            both = jnp.sum(total([(ad[k][i], had[k][j]) for k in range(6)]), axis=0, keepdims=True)
            if h[i][j] is not None:
                both = both + jnp.sum(h[i][j], axis=1, keepdims=True)
            diag = jnp.where(eye, both, 0.0)
            matrix_ref[rows, cols] = diag[:, :WIN]
    wide[: 6 * WIN, : 6 * WIN] = wide[: 6 * WIN, : 6 * WIN] - hl
    flipped = wide[...].T
    matrix_ref[: 6 * WIN, : 6 * WIN] = (
        matrix_ref[: 6 * WIN, : 6 * WIN] - hh + wide[: 6 * WIN, : 6 * WIN] + flipped[: 6 * WIN, : 6 * WIN]
    )
    r = [rc[j] for j in range(6)]
    back = adj_t(rel, cor, r)
    for j in range(6):
        here = jnp.sum(jnp.where(eye, jnp.sum(r[j], axis=1, keepdims=True), 0.0) - back[j], axis=0, keepdims=True)
        matrix_ref[6 * WIN : 6 * WIN + 1, j * WIN : (j + 1) * WIN] = here[:, :WIN]


def finish(me_ref, all_ref, zh_ref, zl_ref, base_ref, scale_ref, pose_ref, step_ref, flat, cols_ref, step3):
    count = all_ref.shape[0]
    f_dev, pix = step_ref.shape
    width = all_ref.shape[2]
    size = 6 * WIN
    shape = (count, width)
    frame = iota(shape, 1) % WIN
    window = iota(shape, 0)
    below = (frame < f_dev) & (window > 0)
    above = (frame >= WIN - f_dev) & (window < count - 1)
    own = (frame >= RADIUS) & (frame < RADIUS + f_dev)

    def settle(x):
        down = pltpu.roll(pltpu.roll(x, 1, 0), width - f_dev, 1)
        up = pltpu.roll(pltpu.roll(x, count - 1, 0), f_dev, 1)
        return x + jnp.where(below, down, 0.0) + jnp.where(above, up, 0.0)

    def dot(x, y):
        return jnp.sum(jnp.where(own, x * y, 0.0), keepdims=True)

    def product(x):
        flat[0:count, :] = x
        tall = flat[...].T
        for w in range(count):
            cols_ref[...] = jnp.broadcast_to(tall[:size, w : w + 1], (size, L))
            pieces = []
            for lt in range(width // L):
                pieces.append(
                    jnp.sum(all_ref[w, :size, lt * L : (lt + 1) * L] * cols_ref[...], axis=0, keepdims=True)
                )
            flat[w : w + 1, :] = jnp.concatenate(pieces, axis=1)
        return settle(flat[0:count, :]) + REG * x

    flat[...] = jnp.zeros_like(flat)
    for w in range(count):
        flat[w : w + 1, :] = all_ref[w, size : size + 1, :]
    residual = settle(flat[0:count, :])
    x = jnp.zeros_like(residual)
    direction = residual
    rr = dot(residual, residual)
    for _ in range(ITERS):
        image = product(direction)
        alpha = rr / dot(direction, image)
        x = x + alpha * direction
        residual = residual - alpha * image
        new = dot(residual, residual)
        direction = residual + (new / rr) * direction
        rr = new
    flat[0:count, :] = x
    mine = flat[pl.ds(me_ref[0], 1), :]
    pose_ref[...] = jnp.broadcast_to(mine, pose_ref.shape)
    cols_ref[...] = jnp.broadcast_to(mine, (L, width)).T[:size]

    @pl.loop(0, f_dev)
    def per_source(s):
        for tile in range(pix // L):
            zcols = pl.ds(pl.multiple_of(s * pix + tile * L, L), L)
            z = zh_ref[:, zcols].astype(F32) + zl_ref[:, zcols].astype(F32)
            image = jnp.sum(z * cols_ref[...], axis=0, keepdims=True)
            here = (tile, pl.ds(s, 1), slice(None))
            step3[here] = base_ref[here] - scale_ref[here] * image

    for tile in range(pix // L):
        step_ref[:, tile * L : (tile + 1) * L] = step3[tile]


def call(body, out, scratch, smem, count):
    vm = pl.BlockSpec(memory_space=pltpu.VMEM)
    sm = pl.BlockSpec(memory_space=pltpu.SMEM)
    return pl.pallas_call(
        body,
        out_shape=[jax.ShapeDtypeStruct(s, t) for s, t in out],
        in_specs=[sm] * smem + [vm] * count,
        out_specs=[vm] * len(out),
        scratch_shapes=scratch,
        compiler_params=pltpu.CompilerParams(vmem_limit_bytes=VMEM_LIMIT),
    )


def shift(block, axis, distance):
    devices = range(lax.axis_size(axis))
    route = [(i - distance, i) for i in devices if i - distance in devices]
    return lax.ppermute(block, axis, route)


def per_device(edge_frames, rotvec, trans, inv_depth, depth_damping, flow, weight, mask):
    f_dev, pix = inv_depth.shape
    edges = mask.shape[0]
    tiles = pix // L
    me = lax.axis_index("frames")
    start = me * f_dev
    source = edge_frames[0] - start + RADIUS
    target = edge_frames[1] - start + RADIUS
    own_rows = f_dev * SLOT
    side = 40
    s = source - RADIUS
    mine = s * SLOT + target - (s // 8) * 8
    i = source
    q = target - 8
    tile = jnp.where(i <= 3, i, jnp.where(i == 7, 4, 6 - i))
    line = jnp.where((i > 3) & (i < 7), q + 7 - i, q)
    lowest = own_rows + tile * 8 + line
    i = source - f_dev - RADIUS
    q = target - f_dev
    tile = jnp.where(i == 0, 4, jnp.where(i <= 4, i - 1, 7 - i))
    line = jnp.where(i > 4, q - i, q)
    highest = own_rows + side + tile * 8 + line
    dest = jnp.where(source < RADIUS, lowest, jnp.where(source >= RADIUS + f_dev, highest, mine))

    def flat(x):
        return x.reshape(edges, 2, tiles, L).transpose(0, 2, 1, 3).reshape(edges * 2 * tiles, L)

    own, low, high = call(
        aggregate,
        [((4, own_rows, pix), F32), ((4, side, pix), F32), ((4, side, pix), F32)],
        [], 0, 4,
    )(dest.reshape(1, edges), flat(flow), flat(weight), mask)
    low = shift(low, "frames", -1)
    high = shift(high, "frames", 1)
    pose = jnp.pad(jnp.concatenate([rotvec, trans], axis=0), ((0, 0), (RADIUS, RADIUS)))
    pose = lax.dynamic_slice_in_dim(pose, start, WIN, axis=1)
    pose = jnp.broadcast_to(pose[:, :, None], (6, WIN, L))
    first = (lax.axis_index("pix") * pix).reshape(1).astype(jnp.int32)
    n = len(UPPER)
    width = 256
    matrix, zh, zl, base, scale = call(
        build,
        [
            ((6 * WIN + 8, width), F32),
            ((6 * WIN, f_dev * pix), BF16),
            ((6 * WIN, f_dev * pix), BF16),
            ((tiles, f_dev, L), F32),
            ((tiles, f_dev, L), F32),
        ],
        [
            pltpu.VMEM((12, WIN, L), F32),
            pltpu.VMEM((21, SLOT, L), F32),
            pltpu.VMEM((n, SLOT, L), F32),
            pltpu.VMEM((6, SLOT, L), F32),
            pltpu.VMEM((n, WIN, L), F32),
            pltpu.VMEM((6, WIN, L), F32),
            pltpu.VMEM((18, WIN, L), F32),
            pltpu.VMEM((256, 256), F32),
            pltpu.VMEM((tiles, f_dev, L), F32),
            pltpu.VMEM((tiles, f_dev, L), F32),
        ],
        1, 6,
    )(first, pose, own, low, high, inv_depth, depth_damping)
    matrix = lax.all_gather(lax.psum(matrix, "pix"), "frames")
    count = lax.axis_size("frames")
    x, step = call(
        finish,
        [((8, width), F32), ((f_dev, pix), F32)],
        [pltpu.VMEM((L, width), F32), pltpu.VMEM((6 * WIN, L), F32), pltpu.VMEM((tiles, f_dev, L), F32)],
        1, 5,
    )(me.reshape(1).astype(jnp.int32), matrix, zh, zl, base, scale)
    return (x[0].reshape(8, WIN)[:6, RADIUS : RADIUS + f_dev], step)


def solution(mesh):
    return jax.shard_map(
        per_device,
        mesh=mesh,
        in_specs=(
            P(None, "frames"),
            P(),
            P(),
            P("frames", "pix"),
            P("frames", "pix"),
            P("frames", None, "pix"),
            P("frames", None, "pix"),
            P("frames", "pix"),
        ),
        out_specs=(P(None, "frames"), P("frames", "pix")),
        check_vma=False,
    )
```

profile of v0, /device:TPU:0, one launch (start us, length us, event | category | flops | bytes accessed | tf_op | source)
XLA Modules:
  0.0 150.0 jit_solution(8673574631069200799)
XLA Ops:
  7.2 0.0 all-reduce.3.cloned.1.call-start
  7.2 1.4 copy.16
  8.6 0.2 reshape.26
  8.8 0.0 copy-start
  8.8 1.9 %copy.17 = f32[192,6,2,128]{3,2,1,0:T(2,128)} copy(f32[192,6,2,128]{3,1,0,2:T(8,128)S(1)} %bitcast.11) | data formatting | bytes 2359296 | tf_op jit(solution)/shard_map/transpose | solution.py:414
  10.7 0.0 copy-done
  10.7 0.1 copy.18
  10.8 0.2 reshape.28
  11.0 0.0 copy-start.3
  11.0 1.9 %copy.19 = f32[192,6,2,128]{3,2,1,0:T(2,128)} copy(f32[192,6,2,128]{3,1,0,2:T(8,128)S(1)} %bitcast.12) | data formatting | bytes 2359296 | tf_op jit(solution)/shard_map/transpose | solution.py:414
  12.9 0.0 copy-done.3
  12.9 0.6 compare_select_fusion.6.dest_ref
  13.5 5.9 %shard_map.95 = (f32[4,384,768]{2,1,0:T(8,128)}, f32[4,40,768]{2,1,0:T(8,128)}, f32[4,40,768]{2,1,0:T(8,128)}) custom-call(s32[1,192]{1,0:T(1,128)} %compare_select_fusion.6.dest_ref, f32[2304,128]{1,0:T(8,128)} %bitcast.13, f32[2304,128]{1,0:T(8,128)} %bitcast.14, s32[192,768]{1,0:T(8,128)} %mask_ref.1), custom_call_target="tpu_custom_call" | custom-call | tf_op jit(solution)/shard_map/pallas_call | solution.py:416
  19.4 1.3 collective-permute-start
  20.7 3.1 %collective-permute-start.1 = (f32[4,40,768]{2,1,0:T(8,128)}, f32[4,40,768]{2,1,0:T(8,128)S(1)}, u32[]{:S(2)}, u32[]{:S(2)}) collective-permute-start(f32[4,40,768]{2,1,0:T(8,128)} %get-tuple-element.14), channel_id=1, source_target_pairs={{0,4},{4,8},{8,12},{12,16},{16,20},{20,24},{24,28},{1,5},{5,9},{9,... | collective-permute-start | bytes 1474568 | tf_op jit(solution)/shard_map/ppermute | solution.py:386
  23.8 0.0 copy-done.4
  23.8 0.0 copy-done.5
  23.8 0.1 fusion.1
  23.9 0.0 collective-permute-done.low_ref
  23.9 1.5 %collective-permute-done.1.high_ref = f32[4,40,768]{2,1,0:T(8,128)S(1)} collective-permute-done((f32[4,40,768]{2,1,0:T(8,128)}, f32[4,40,768]{2,1,0:T(8,128)S(1)}, u32[]{:S(2)}, u32[]{:S(2)}) %collective-permute-start.1) | collective-permute-done | bytes 491552 | tf_op jit(solution)/shard_map/ppermute | solution.py:386
  25.5 0.8 broadcast_in_dim.11.pose_ref
  26.3 0.0 copy-done.1
  26.3 27.8 %shard_map.96 = (f32[200,256]{1,0:T(8,128)}, bf16[192,12288]{1,0:T(8,128)(2,1)}, bf16[192,12288]{1,0:T(8,128)(2,1)}, f32[6,16,128]{2,1,0:T(8,128)}, f32[6,16,128]{2,1,0:T(8,128)}) custom-call(s32[1]{0:T(128)} %bitcast.1.first_ref, f32[6,32,128]{2,1,0:T(8,128)} %broadcast_in_dim.11.pose_ref, f32[4,384,768]{2,1,0:T(8,128)} %get-tuple-element.12.own_ref, ...), custom_call_target="tpu_custom_call" | custom-call | tf_op jit(solution)/shard_map/pallas_call | solution.py:429
  54.0 0.0 all-reduce.3.cloned.1.call-update
  54.1 0.0 all-gather.2.cloned.1.call-start
  54.1 47.2 %all-reduce.3.cloned.1.call-done = f32[1,200,256]{2,1,0:T(8,128)} async-done(((f32[1,200,256]{2,1,0:T(8,128)}), f32[1,200,256]{2,1,0:T(8,128)}) %all-reduce.3.cloned.1.call-update) | async-done | bytes 204816 | tf_op jit(solution)/shard_map/psum | solution.py:452
  101.4 0.0 all-gather.2.cloned.1.call-update
  101.4 27.8 %all-gather.2.cloned.1.call-done.all_ref = f32[8,200,256]{2,1,0:T(8,128)} async-done(((f32[1,200,256]{2,1,0:T(8,128)}), f32[8,200,256]{2,1,0:T(8,128)}) %all-gather.2.cloned.1.call-update) | async-done | bytes 1638416 | tf_op jit(solution)/shard_map/all_gather | solution.py:452
  129.2 12.5 %shard_map.97 = (f32[8,256]{1,0:T(8,128)}, f32[16,768]{1,0:T(8,128)}) custom-call(s32[1]{0:T(128)} %bitcast.me_ref, f32[8,200,256]{2,1,0:T(8,128)} %all-gather.2.cloned.1.call-done.all_ref, bf16[192,12288]{1,0:T(8,128)(2,1)} %get-tuple-element.16.zh_ref, bf16[192,12288]{1,0:T(8,128)(2,1)} %get-tuple-element.17.zl_ref, ...), custom_call_target="tpu_custom_call" | custom-call | tf_op jit(solution)/shard_map/pallas_call | solution.py:454
  141.7 0.7 slice_reduce_fusion
  142.4 0.1 reshape_squeeze.3
  142.5 0.7 slice.15
  (5 shorter events, 0.0 us)
Async XLA Ops:
  7.2 94.2 %all-reduce.3.cloned.1.call-start = ((), (), s32[]{:S(2)}) async-start(), calls=%async_computation | async-start | bytes 409600 | tf_op jit(solution)/shard_map/psum | solution.py:452
  8.8 1.9 %copy-start = (f32[192,2,768]{2,1,0:T(2,128)S(1)}, f32[192,2,768]{2,1,0:T(2,128)}, u32[]{:S(2)}) copy-start(f32[192,2,768]{2,1,0:T(2,128)} %param.14) | copy-start | bytes 3538948
  11.0 2.0 %copy-start.3 = (s32[2,192]{1,0:T(2,128)S(1)}, s32[2,192]{1,0:T(2,128)}, u32[]{:S(2)}) copy-start(s32[2,192]{1,0:T(2,128)} %param.8) | copy-start | bytes 4612
  12.9 10.9 %copy-start.4 = (f32[3,128]{1,0:T(4,128)S(1)}, f32[3,128]{1,0:T(4,128)}, u32[]{:S(2)}) copy-start(f32[3,128]{1,0:T(4,128)} %param.9) | copy-start | bytes 4612
  12.9 10.9 %copy-start.5 = (f32[3,128]{1,0:T(4,128)S(1)}, f32[3,128]{1,0:T(4,128)}, u32[]{:S(2)}) copy-start(f32[3,128]{1,0:T(4,128)} %param.10) | copy-start | bytes 4612
  19.4 4.5 %collective-permute-start = (f32[4,40,768]{2,1,0:T(8,128)}, f32[4,40,768]{2,1,0:T(8,128)S(1)}, u32[]{:S(2)}, u32[]{:S(2)}) collective-permute-start(f32[4,40,768]{2,1,0:T(8,128)} %get-tuple-element.13), channel_id=1, source_target_pairs={{4,0},{8,4},{12,8},{16,12},{20,16},{24,20},{28,24},{5,1},{9,5},{13... | collective-permute-start | bytes 1474568 | tf_op jit(solution)/shard_map/ppermute | solution.py:386
  20.7 4.7 %collective-permute-start.1 = (f32[4,40,768]{2,1,0:T(8,128)}, f32[4,40,768]{2,1,0:T(8,128)S(1)}, u32[]{:S(2)}, u32[]{:S(2)}) collective-permute-start(f32[4,40,768]{2,1,0:T(8,128)} %get-tuple-element.14), channel_id=1, source_target_pairs={{0,4},{4,8},{8,12},{12,16},{16,20},{20,24},{24,28},{1,5},{5,9},{9,... | collective-permute-start | bytes 1474568 | tf_op jit(solution)/shard_map/ppermute | solution.py:386
  23.9 2.4 %copy-start.1 = (f32[4,40,768]{2,1,0:T(8,128)}, f32[4,40,768]{2,1,0:T(8,128)S(1)}, u32[]{:S(2)}) copy-start(f32[4,40,768]{2,1,0:T(8,128)S(1)} %collective-permute-done.low_ref) | copy-start | bytes 1474564
  25.5 0.8 copy-start.2
  54.1 75.1 %all-gather.2.cloned.1.call-start = ((), (), s32[]{:S(2)}) async-start(), calls=%async_computation.1 | async-start | bytes 1843200 | tf_op jit(solution)/shard_map/all_gather | solution.py:452
Sparse Core Ops, SparseCore 0:
  54.2 47.1 all-reduce.2
  103.2 25.9 all-gather.1
where the time goes:
time: 150 us
  waiting for transfers between devices  76.6 us (51%)
  Pallas kernels  46.2 us (31%)
  between operations  14.1 us (9%)
  local copies, waits for them, and re-layouts  7.95 us (5%)
  starting transfers between devices  4.42 us (3%)
    psum x1, waiting for transfers between devices, per_device(): matrix = lax.all_gather(lax.psum(matrix, 'pix'), 'frames')  47.2 us
    all_gather x1, waiting for transfers between devices, per_device(): matrix = lax.all_gather(lax.psum(matrix, 'pix'), 'frames')  27.8 us
    pallas_call x1, Pallas kernels, per_device(): call(build, [((6 * WIN + 8, width), F32), ((6 * WIN, f_dev * pix), BF16),...  27.8 us
    pallas_call x1, Pallas kernels, per_device(): call(finish, [((8, width), F32), ((f_dev, pix), F32)], [pltpu.VMEM((L, wi...  12.5 us
    pallas_call x1, Pallas kernels, per_device(): call(aggregate, [((4, own_rows, pix), F32), ((4, side, pix), F32), ((4, s...  5.93 us
    ppermute x2, starting transfers between devices, shift(): return lax.ppermute(block, axis, route)  4.34 us
    transpose x2, local copies, waits for them, and re-layouts, flat(): x.reshape(edges, 2, tiles, L).transpose(0, 2, 1, 3)  3.86 us
  transfers between devices with their start and end apart: 4, of which 3 were waited for; matrix products, arithmetic and copies ran while one was open for 0% of the time, Pallas kernels for 0%

commit v1 on v0

--- a/solution.py
+++ b/solution.py
@@ -301,11 +301,63 @@
         matrix_ref[6 * WIN : 6 * WIN + 1, j * WIN : (j + 1) * WIN] = here[:, :WIN]
 
 
-def finish(me_ref, all_ref, zh_ref, zl_ref, base_ref, scale_ref, pose_ref, step_ref, flat, cols_ref, step3):
-    count = all_ref.shape[0]
+def remote(src, dst, sems, phase, which, axis, peer):
+    return pltpu.make_async_remote_copy(
+        src_ref=src,
+        dst_ref=dst,
+        send_sem=sems.at[0, phase, which],
+        recv_sem=sems.at[1, phase, which],
+        device_id={axis: peer},
+        device_id_type=pl.DeviceIdType.MESH,
+    )
+
+
+def peers(axis):
+    count = lax.axis_size(axis)
+    me = lax.axis_index(axis)
+    return [lax.rem(me + step, count) for step in range(1, count)]
+
+
+def finish(
+    matrix_ref, zh_ref, zl_ref, base_ref, scale_ref, pose_ref, step_ref,
+    flat, cols_ref, step3, land, summed, rows_ref, pix_sem, round_sem,
+):
+    count = lax.axis_size("frames")
+    me = lax.axis_index("frames")
     f_dev, pix = step_ref.shape
-    width = all_ref.shape[2]
+    width = matrix_ref.shape[1]
     size = 6 * WIN
+    zcount = lax.axis_size("pix")
+    z = lax.axis_index("pix")
+    chunk = matrix_ref.shape[0] // zcount
+
+    def piece(which):
+        return pl.ds(pl.multiple_of(which * chunk, 8), chunk)
+
+    sent = []
+    for peer in peers("pix"):
+        copy = remote(matrix_ref.at[piece(peer)], land.at[z], pix_sem, 0, len(sent), "pix", peer)
+        copy.start()
+        sent.append(copy)
+    land[z] = matrix_ref[piece(z), :]
+    for copy in sent:
+        copy.wait_recv()
+    reduced = land[0]
+    for k in range(1, zcount):
+        reduced = reduced + land[k]
+    for copy in sent:
+        copy.wait_send()
+    summed[piece(z), :] = reduced
+    sent = []
+    for peer in peers("pix"):
+        copy = remote(summed.at[piece(z)], summed.at[piece(z)], pix_sem, 1, len(sent), "pix", peer)
+        copy.start()
+        sent.append(copy)
+    for copy in sent:
+        copy.wait_recv()
+    for copy in sent:
+        copy.wait_send()
+
     shape = (count, width)
     frame = iota(shape, 1) % WIN
     window = iota(shape, 0)
@@ -321,28 +373,38 @@
     def dot(x, y):
         return jnp.sum(jnp.where(own, x * y, 0.0), keepdims=True)
 
-    def product(x):
+    def gather(step, row):
+        rows_ref[step, me] = row
+        sent = []
+        here = rows_ref.at[step, me]
+        for peer in peers("frames"):
+            copy = remote(here, here, round_sem, step, len(sent), "frames", peer)
+            copy.start()
+            sent.append(copy)
+        for copy in sent:
+            copy.wait_recv()
+        for w in range(count):
+            flat[w : w + 1, :] = rows_ref[step, w]
+        for copy in sent:
+            copy.wait_send()
+        return settle(flat[0:count, :])
+
+    def product(step, x):
         flat[0:count, :] = x
-        tall = flat[...].T
-        for w in range(count):
-            cols_ref[...] = jnp.broadcast_to(tall[:size, w : w + 1], (size, L))
-            pieces = []
-            for lt in range(width // L):
-                pieces.append(
-                    jnp.sum(all_ref[w, :size, lt * L : (lt + 1) * L] * cols_ref[...], axis=0, keepdims=True)
-                )
-            flat[w : w + 1, :] = jnp.concatenate(pieces, axis=1)
-        return settle(flat[0:count, :]) + REG * x
-
-    flat[...] = jnp.zeros_like(flat)
-    for w in range(count):
-        flat[w : w + 1, :] = all_ref[w, size : size + 1, :]
-    residual = settle(flat[0:count, :])
+        cols_ref[...] = jnp.broadcast_to(flat[pl.ds(me, 1), :], (L, width)).T[:size]
+        pieces = []
+        for lt in range(width // L):
+            pieces.append(
+                jnp.sum(summed[:size, lt * L : (lt + 1) * L] * cols_ref[...], axis=0, keepdims=True)
+            )
+        return gather(step, jnp.concatenate(pieces, axis=1)) + REG * x
+
+    residual = gather(0, summed[size : size + 1, :])
     x = jnp.zeros_like(residual)
     direction = residual
     rr = dot(residual, residual)
-    for _ in range(ITERS):
-        image = product(direction)
+    for step in range(ITERS):
+        image = product(step + 1, direction)
         alpha = rr / dot(direction, image)
         x = x + alpha * direction
         residual = residual - alpha * image
@@ -350,7 +412,7 @@
         direction = residual + (new / rr) * direction
         rr = new
     flat[0:count, :] = x
-    mine = flat[pl.ds(me_ref[0], 1), :]
+    mine = flat[pl.ds(me, 1), :]
     pose_ref[...] = jnp.broadcast_to(mine, pose_ref.shape)
     cols_ref[...] = jnp.broadcast_to(mine, (L, width)).T[:size]
 
@@ -367,7 +429,25 @@
         step_ref[:, tile * L : (tile + 1) * L] = step3[tile]
 
 
-def call(body, out, scratch, smem, count):
+def solve(first_ref, pose_ref, own_ref, low_ref, high_ref, depth_ref, damp_ref, x_ref, step_ref, *scratch):
+    matrix, zh, zl, base, scale = scratch[:5]
+    barrier = pltpu.get_barrier_semaphore()
+    total = 0
+    for axis in ("frames", "pix"):
+        for peer in peers(axis):
+            pl.semaphore_signal(
+                barrier, inc=1, device_id={axis: peer}, device_id_type=pl.DeviceIdType.MESH
+            )
+            total += 1
+    build(
+        first_ref, pose_ref, own_ref, low_ref, high_ref, depth_ref, damp_ref,
+        matrix, zh, zl, base, scale, *scratch[5:15],
+    )
+    pl.semaphore_wait(barrier, total)
+    finish(matrix, zh, zl, base, scale, x_ref, step_ref, *scratch[15:])
+
+
+def call(body, out, scratch, smem, count, **params):
     vm = pl.BlockSpec(memory_space=pltpu.VMEM)
     sm = pl.BlockSpec(memory_space=pltpu.SMEM)
     return pl.pallas_call(
@@ -376,7 +456,7 @@
         in_specs=[sm] * smem + [vm] * count,
         out_specs=[vm] * len(out),
         scratch_shapes=scratch,
-        compiler_params=pltpu.CompilerParams(vmem_limit_bytes=VMEM_LIMIT),
+        compiler_params=pltpu.CompilerParams(vmem_limit_bytes=VMEM_LIMIT, **params),
     )
 
 
@@ -426,16 +506,18 @@
     first = (lax.axis_index("pix") * pix).reshape(1).astype(jnp.int32)
     n = len(UPPER)
     width = 256
-    matrix, zh, zl, base, scale = call(
-        build,
+    count = lax.axis_size("frames")
+    zcount = lax.axis_size("pix")
+    chunk = -(-(6 * WIN + 8) // (8 * zcount)) * 8
+    x, step = call(
+        solve,
+        [((8, width), F32), ((f_dev, pix), F32)],
         [
-            ((6 * WIN + 8, width), F32),
-            ((6 * WIN, f_dev * pix), BF16),
-            ((6 * WIN, f_dev * pix), BF16),
-            ((tiles, f_dev, L), F32),
-            ((tiles, f_dev, L), F32),
-        ],
-        [
+            pltpu.VMEM((chunk * zcount, width), F32),
+            pltpu.VMEM((6 * WIN, f_dev * pix), BF16),
+            pltpu.VMEM((6 * WIN, f_dev * pix), BF16),
+            pltpu.VMEM((tiles, f_dev, L), F32),
+            pltpu.VMEM((tiles, f_dev, L), F32),
             pltpu.VMEM((12, WIN, L), F32),
             pltpu.VMEM((21, SLOT, L), F32),
             pltpu.VMEM((n, SLOT, L), F32),
@@ -446,17 +528,17 @@
             pltpu.VMEM((256, 256), F32),
             pltpu.VMEM((tiles, f_dev, L), F32),
             pltpu.VMEM((tiles, f_dev, L), F32),
+            pltpu.VMEM((L, width), F32),
+            pltpu.VMEM((6 * WIN, L), F32),
+            pltpu.VMEM((tiles, f_dev, L), F32),
+            pltpu.VMEM((zcount, chunk, width), F32),
+            pltpu.VMEM((chunk * zcount, width), F32),
+            pltpu.VMEM((ITERS + 1, count, 1, width), F32),
+            pltpu.SemaphoreType.DMA((2, 2, zcount)),
+            pltpu.SemaphoreType.DMA((2, ITERS + 1, count)),
         ],
-        1, 6,
+        1, 6, collective_id=0, has_side_effects=True,
     )(first, pose, own, low, high, inv_depth, depth_damping)
-    matrix = lax.all_gather(lax.psum(matrix, "pix"), "frames")
-    count = lax.axis_size("frames")
-    x, step = call(
-        finish,
-        [((8, width), F32), ((f_dev, pix), F32)],
-        [pltpu.VMEM((L, width), F32), pltpu.VMEM((6 * WIN, L), F32), pltpu.VMEM((tiles, f_dev, L), F32)],
-        1, 5,
-    )(me.reshape(1).astype(jnp.int32), matrix, zh, zl, base, scale)
     return (x[0].reshape(8, WIN)[:6, RADIUS : RADIUS + f_dev], step)
 
 

time: 150 us -> 101 us (0.67)
  waiting for transfers between devices: 76.6 us -> 1.54 us
  Pallas kernels: 46.2 us -> 84.2 us
  between operations: 14.1 us -> 0.74 us
  local copies, waits for them, and re-layouts: 7.95 us -> 9.47 us
    psum x1 -> x0, waiting for transfers between devices: 47.2 us -> none  [per_device(): matrix = lax.all_gather(lax.psum(matrix, 'pix'), 'frames')]
    pallas_call x2 -> x1, Pallas kernels: 40.3 us -> 78.2 us  [per_device(): call(solve, [((8, width), F32), ((f_dev, pix), F32)], [pltpu.VMEM((chunk...]
    all_gather x1 -> x0, waiting for transfers between devices: 27.8 us -> none  [per_device(): matrix = lax.all_gather(lax.psum(matrix, 'pix'), 'frames')]
  transfers between devices with their start and end apart: 4 -> 2, of which waited for: 3 -> 1; matrix products, arithmetic and copies ran while one was open for 0% -> 0% of each run, Pallas kernels for 0% -> 0%
where the time goes in v1:
time: 101 us
  Pallas kernels  84.2 us (83%)
  local copies, waits for them, and re-layouts  9.47 us (9%)
  starting transfers between devices  4.34 us (4%)
  waiting for transfers between devices  1.54 us (2%)
    pallas_call x1, Pallas kernels, per_device(): call(solve, [((8, width), F32), ((f_dev, pix), F32)], [pltpu.VMEM((chunk...  78.2 us
    pallas_call x1, Pallas kernels, per_device(): call(aggregate, [((4, own_rows, pix), F32), ((4, side, pix), F32), ((4, s...  5.95 us
    ppermute x2, starting transfers between devices, shift(): return lax.ppermute(block, axis, route)  4.34 us
    transpose x2, local copies, waits for them, and re-layouts, flat(): x.reshape(edges, 2, tiles, L).transpose(0, 2, 1, 3)  3.93 us
    unnamed x15, local copies, waits for them, and re-layouts  2.88 us
  transfers between devices with their start and end apart: 2, of which 1 were waited for; matrix products, arithmetic and copies ran while one was open for 0% of the time, Pallas kernels for 0%

profile of v1, /device:TPU:0, one launch (start us, length us, event | category | flops | bytes accessed | tf_op | source)
XLA Modules:
  0.0 101.0 jit_solution(12559056925996907602)
XLA Ops:
  0.6 1.4 %copy.12 = f32[192,2,768]{2,0,1:T(8,128)S(1)} copy(f32[192,2,768]{2,1,0:T(2,128)} %param.13) | data formatting | bytes 2359296 | tf_op args[5]
  2.0 0.2 reshape.22
  2.2 0.0 copy-start
  2.2 2.0 %copy.13 = f32[192,6,2,128]{3,2,1,0:T(2,128)} copy(f32[192,6,2,128]{3,1,0,2:T(8,128)S(1)} %bitcast.9) | data formatting | bytes 2359296 | tf_op jit(solution)/shard_map/transpose | solution.py:494
  4.2 0.0 copy-done
  4.2 0.1 copy.14
  4.3 0.2 reshape.24
  4.5 0.0 copy-start.3
  4.5 2.0 %copy.15 = f32[192,6,2,128]{3,2,1,0:T(2,128)} copy(f32[192,6,2,128]{3,1,0,2:T(8,128)S(1)} %bitcast.10) | data formatting | bytes 2359296 | tf_op jit(solution)/shard_map/transpose | solution.py:494
  6.4 0.0 copy-done.3
  6.4 0.6 compare_select_fusion.6.dest_ref
  7.0 0.0 copy-start.4
  7.0 0.0 copy-start.5
  7.0 6.0 %shard_map.95 = (f32[4,384,768]{2,1,0:T(8,128)}, f32[4,40,768]{2,1,0:T(8,128)}, f32[4,40,768]{2,1,0:T(8,128)}) custom-call(s32[1,192]{1,0:T(1,128)} %compare_select_fusion.6.dest_ref, f32[2304,128]{1,0:T(8,128)} %bitcast.11, f32[2304,128]{1,0:T(8,128)} %bitcast.12, s32[192,768]{1,0:T(8,128)} %mask_ref.1), custom_call_target="tpu_custom_call" | custom-call | tf_op jit(solution)/shard_map/pallas_call | solution.py:496
  13.0 1.3 %collective-permute-start = (f32[4,40,768]{2,1,0:T(8,128)}, f32[4,40,768]{2,1,0:T(8,128)S(1)}, u32[]{:S(2)}, u32[]{:S(2)}) collective-permute-start(f32[4,40,768]{2,1,0:T(8,128)} %get-tuple-element.8), channel_id=1, source_target_pairs={{4,0},{8,4},{12,8},{16,12},{20,16},{24,20},{28,24},{5,1},{9,5},{13... | collective-permute-start | bytes 1474568 | tf_op jit(solution)/shard_map/ppermute | solution.py:466
  14.2 3.1 %collective-permute-start.1 = (f32[4,40,768]{2,1,0:T(8,128)}, f32[4,40,768]{2,1,0:T(8,128)S(1)}, u32[]{:S(2)}, u32[]{:S(2)}) collective-permute-start(f32[4,40,768]{2,1,0:T(8,128)} %get-tuple-element.9), channel_id=1, source_target_pairs={{0,4},{4,8},{8,12},{12,16},{16,20},{20,24},{24,28},{1,5},{5,9},{9,... | collective-permute-start | bytes 1474568 | tf_op jit(solution)/shard_map/ppermute | solution.py:466
  17.3 0.0 copy-done.4
  17.3 0.0 copy-done.5
  17.3 0.1 fusion.1
  17.4 0.0 collective-permute-done.low_ref
  17.4 0.0 copy-start.1
  17.4 1.5 %collective-permute-done.1.high_ref = f32[4,40,768]{2,1,0:T(8,128)S(1)} collective-permute-done((f32[4,40,768]{2,1,0:T(8,128)}, f32[4,40,768]{2,1,0:T(8,128)S(1)}, u32[]{:S(2)}, u32[]{:S(2)}) %collective-permute-start.1) | collective-permute-done | bytes 491552 | tf_op jit(solution)/shard_map/ppermute | solution.py:466
  19.0 0.0 copy-start.2
  19.0 0.8 broadcast_in_dim.11.pose_ref
  19.8 0.0 copy-done.1
  19.8 0.0 copy-done.2
  19.8 78.2 %shard_map.96 = (f32[8,256]{1,0:T(8,128)}, f32[16,768]{1,0:T(8,128)}) custom-call(s32[1]{0:T(128)} %bitcast.first_ref, f32[6,32,128]{2,1,0:T(8,128)} %broadcast_in_dim.11.pose_ref, f32[4,384,768]{2,1,0:T(8,128)} %get-tuple-element.7.own_ref, f32[4,40,768]{2,1,0:T(8,128)} %copy-done.1, f32[4,40,768]{2,1,0:T(8,128)} %copy-done.2, f32[16,768]{1,0:T(8,128)} %depth_ref.1, ...), custom_call_target="tpu_custom_call" | custom-call | tf_op jit(solution)/shard_map/pallas_call | solution.py:512
  98.1 0.7 slice_reduce_fusion
  98.8 0.1 reshape_squeeze.3
  98.9 0.7 slice.15
  99.5 1.4 %copy.17 = f32[16,768]{1,0:T(8,128)} copy(f32[16,768]{1,0:T(8,128)} %get-tuple-element.15) | data formatting | bytes 98304
Async XLA Ops:
  2.2 2.0 %copy-start = (f32[192,2,768]{2,1,0:T(2,128)S(1)}, f32[192,2,768]{2,1,0:T(2,128)}, u32[]{:S(2)}) copy-start(f32[192,2,768]{2,1,0:T(2,128)} %param.14) | copy-start | bytes 3538948
  4.5 2.0 %copy-start.3 = (s32[2,192]{1,0:T(2,128)S(1)}, s32[2,192]{1,0:T(2,128)}, u32[]{:S(2)}) copy-start(s32[2,192]{1,0:T(2,128)} %param.8) | copy-start | bytes 4612
  7.0 10.3 %copy-start.4 = (f32[3,128]{1,0:T(4,128)S(1)}, f32[3,128]{1,0:T(4,128)}, u32[]{:S(2)}) copy-start(f32[3,128]{1,0:T(4,128)} %param.9) | copy-start | bytes 4612
  7.0 10.3 %copy-start.5 = (f32[3,128]{1,0:T(4,128)S(1)}, f32[3,128]{1,0:T(4,128)}, u32[]{:S(2)}) copy-start(f32[3,128]{1,0:T(4,128)} %param.10) | copy-start | bytes 4612
  13.0 4.5 %collective-permute-start = (f32[4,40,768]{2,1,0:T(8,128)}, f32[4,40,768]{2,1,0:T(8,128)S(1)}, u32[]{:S(2)}, u32[]{:S(2)}) collective-permute-start(f32[4,40,768]{2,1,0:T(8,128)} %get-tuple-element.8), channel_id=1, source_target_pairs={{4,0},{8,4},{12,8},{16,12},{20,16},{24,20},{28,24},{5,1},{9,5},{13... | collective-permute-start | bytes 1474568 | tf_op jit(solution)/shard_map/ppermute | solution.py:466
  14.2 4.7 %collective-permute-start.1 = (f32[4,40,768]{2,1,0:T(8,128)}, f32[4,40,768]{2,1,0:T(8,128)S(1)}, u32[]{:S(2)}, u32[]{:S(2)}) collective-permute-start(f32[4,40,768]{2,1,0:T(8,128)} %get-tuple-element.9), channel_id=1, source_target_pairs={{0,4},{4,8},{8,12},{12,16},{16,20},{20,24},{24,28},{1,5},{5,9},{9,... | collective-permute-start | bytes 1474568 | tf_op jit(solution)/shard_map/ppermute | solution.py:466
  17.4 2.4 %copy-start.1 = (f32[4,40,768]{2,1,0:T(8,128)}, f32[4,40,768]{2,1,0:T(8,128)S(1)}, u32[]{:S(2)}) copy-start(f32[4,40,768]{2,1,0:T(8,128)S(1)} %collective-permute-done.low_ref) | copy-start | bytes 1474564
  19.0 0.8 copy-start.2

commit v2 on v1

--- a/solution.py
+++ b/solution.py
@@ -429,7 +429,10 @@
         step_ref[:, tile * L : (tile + 1) * L] = step3[tile]
 
 
-def solve(first_ref, pose_ref, own_ref, low_ref, high_ref, depth_ref, damp_ref, x_ref, step_ref, *scratch):
+def solve(
+    first_ref, dest_ref, flow_ref, weight_ref, mask_ref, pose_ref, depth_ref, damp_ref,
+    x_ref, step_ref, own_ref, low_out, high_out, low_ref, high_ref, edge_sem, *scratch,
+):
     matrix, zh, zl, base, scale = scratch[:5]
     barrier = pltpu.get_barrier_semaphore()
     total = 0
@@ -439,11 +442,21 @@
                 barrier, inc=1, device_id={axis: peer}, device_id_type=pl.DeviceIdType.MESH
             )
             total += 1
+    aggregate(dest_ref, flow_ref, weight_ref, mask_ref, own_ref, low_out, high_out)
+    pl.semaphore_wait(barrier, total)
+    around = peers("frames")
+    edge = [
+        remote(low_out, low_ref, edge_sem, 0, 0, "frames", around[-1]),
+        remote(high_out, high_ref, edge_sem, 1, 0, "frames", around[0]),
+    ]
+    for copy in edge:
+        copy.start()
+    for copy in edge:
+        copy.wait()
     build(
         first_ref, pose_ref, own_ref, low_ref, high_ref, depth_ref, damp_ref,
         matrix, zh, zl, base, scale, *scratch[5:15],
     )
-    pl.semaphore_wait(barrier, total)
     finish(matrix, zh, zl, base, scale, x_ref, step_ref, *scratch[15:])
 
 
@@ -458,12 +471,6 @@
         scratch_shapes=scratch,
         compiler_params=pltpu.CompilerParams(vmem_limit_bytes=VMEM_LIMIT, **params),
     )
-
-
-def shift(block, axis, distance):
-    devices = range(lax.axis_size(axis))
-    route = [(i - distance, i) for i in devices if i - distance in devices]
-    return lax.ppermute(block, axis, route)
 
 
 def per_device(edge_frames, rotvec, trans, inv_depth, depth_damping, flow, weight, mask):
@@ -493,13 +500,6 @@
     def flat(x):
         return x.reshape(edges, 2, tiles, L).transpose(0, 2, 1, 3).reshape(edges * 2 * tiles, L)
 
-    own, low, high = call(
-        aggregate,
-        [((4, own_rows, pix), F32), ((4, side, pix), F32), ((4, side, pix), F32)],
-        [], 0, 4,
-    )(dest.reshape(1, edges), flat(flow), flat(weight), mask)
-    low = shift(low, "frames", -1)
-    high = shift(high, "frames", 1)
     pose = jnp.pad(jnp.concatenate([rotvec, trans], axis=0), ((0, 0), (RADIUS, RADIUS)))
     pose = lax.dynamic_slice_in_dim(pose, start, WIN, axis=1)
     pose = jnp.broadcast_to(pose[:, :, None], (6, WIN, L))
@@ -513,6 +513,12 @@
         solve,
         [((8, width), F32), ((f_dev, pix), F32)],
         [
+            pltpu.VMEM((4, own_rows, pix), F32),
+            pltpu.VMEM((4, side, pix), F32),
+            pltpu.VMEM((4, side, pix), F32),
+            pltpu.VMEM((4, side, pix), F32),
+            pltpu.VMEM((4, side, pix), F32),
+            pltpu.SemaphoreType.DMA((2, 2, 1)),
             pltpu.VMEM((chunk * zcount, width), F32),
             pltpu.VMEM((6 * WIN, f_dev * pix), BF16),
             pltpu.VMEM((6 * WIN, f_dev * pix), BF16),
@@ -537,8 +543,11 @@
             pltpu.SemaphoreType.DMA((2, 2, zcount)),
             pltpu.SemaphoreType.DMA((2, ITERS + 1, count)),
         ],
-        1, 6, collective_id=0, has_side_effects=True,
-    )(first, pose, own, low, high, inv_depth, depth_damping)
+        1, 7, collective_id=0, has_side_effects=True,
+    )(
+        first, dest.reshape(1, edges), flat(flow), flat(weight), mask,
+        pose, inv_depth, depth_damping,
+    )
     return (x[0].reshape(8, WIN)[:6, RADIUS : RADIUS + f_dev], step)
 
 

time: 101 us -> 95.7 us (0.948)
  starting transfers between devices: 4.34 us -> 0 us
  waiting for transfers between devices: 1.54 us -> 0 us
    ppermute x2 -> x0, starting transfers between devices: 4.34 us -> none  [shift(): return lax.ppermute(block, axis, route)]
    ppermute x2 -> x0, waiting for transfers between devices: 1.54 us -> none  [shift(): return lax.ppermute(block, axis, route)]
    pallas_call x2 -> x1, Pallas kernels: 84.2 us -> 84 us  [per_device(): call(solve, [((8, width), F32), ((f_dev, pix), F32)], [pltpu.VMEM((4, own...]
    unnamed x15 -> x9, local copies, waits for them, and re-layouts: 2.88 us -> 2.87 us
  transfers between devices with their start and end apart: 2 -> 0, of which waited for: 1 -> 0; matrix products, arithmetic and copies ran while one was open for 0% -> 0% of each run, Pallas kernels for 0% -> 0%
where the time goes in v2:
time: 95.7 us; the launch traced here: 95.4 us
  Pallas kernels  84 us (88%)
  local copies, waits for them, and re-layouts  9.3 us (10%)
  other arithmetic  1.42 us (1%)
    pallas_call x1, Pallas kernels, per_device(): call(solve, [((8, width), F32), ((f_dev, pix), F32)], [pltpu.VMEM((4, own...  84 us
    transpose x2, local copies, waits for them, and re-layouts, flat(): x.reshape(edges, 2, tiles, L).transpose(0, 2, 1, 3)  3.89 us
    unnamed x9, local copies, waits for them, and re-layouts  2.87 us

profile of v2, /device:TPU:0, one launch (start us, length us, event | category | flops | bytes accessed | tf_op | source)
XLA Modules:
  0.0 95.4 jit_solution(10809281883738026195)
XLA Ops:
  0.6 1.3 %compare_select_fusion.6.dest_ref = s32[1,192]{1,0:T(1,128)} fusion(s32[2,192]{1,0:T(2,128)} %param.8, s32[]{:T(128)S(6)} %mul.23), kind=kLoop, calls=%fused_computation.17 | loop fusion | flops 10560 | bytes 2308 | tf_op jit(solution)/shard_map/jit(_where)/select_n | solution.py:498
  2.0 1.3 %copy.12 = f32[192,2,768]{2,0,1:T(8,128)S(1)} copy(f32[192,2,768]{2,1,0:T(2,128)} %param.13) | data formatting | bytes 2359296 | tf_op args[5]
  3.3 0.2 reshape.22
  3.5 0.0 copy-start
  3.5 1.9 %copy.13 = f32[192,6,2,128]{3,2,1,0:T(2,128)} copy(f32[192,6,2,128]{3,1,0,2:T(8,128)S(1)} %bitcast.9) | data formatting | bytes 2359296 | tf_op jit(solution)/shard_map/transpose | solution.py:501
  5.5 0.0 copy-done
  5.5 0.1 copy.14
  5.5 0.2 reshape.24
  5.7 0.0 copy-start.1
  5.7 0.0 copy-start.2
  5.8 2.0 %copy.15 = f32[192,6,2,128]{3,2,1,0:T(2,128)} copy(f32[192,6,2,128]{3,1,0,2:T(8,128)S(1)} %bitcast.10) | data formatting | bytes 2359296 | tf_op jit(solution)/shard_map/transpose | solution.py:501
  7.7 0.0 copy-done.1
  7.7 0.0 copy-done.2
  7.7 0.1 fusion.1
  7.8 0.7 broadcast_in_dim.12.pose_ref
  8.5 84.0 %shard_map.95 = (f32[8,256]{1,0:T(8,128)}, f32[16,768]{1,0:T(8,128)}) custom-call(s32[1]{0:T(128)} %bitcast.first_ref, s32[1,192]{1,0:T(1,128)} %compare_select_fusion.6.dest_ref, f32[2304,128]{1,0:T(8,128)} %bitcast.11, f32[2304,128]{1,0:T(8,128)} %bitcast.12, s32[192,768]{1,0:T(8,128)} %mask_ref.1, f32[6,32,128]{2,1,0:T(8,128)} %broadcast_in_dim.12.pose_ref, ...), custom_call_target="tpu_custom_call" | custom-call | tf_op jit(solution)/shard_map/pallas_call | solution.py:512
  92.5 0.7 slice_reduce_fusion
  93.3 0.1 reshape_squeeze.3
  93.3 0.7 slice.15
  94.0 1.4 %copy.17 = f32[16,768]{1,0:T(8,128)} copy(f32[16,768]{1,0:T(8,128)} %get-tuple-element.9) | data formatting | bytes 98304
Async XLA Ops:
  3.5 1.9 %copy-start = (f32[192,2,768]{2,1,0:T(2,128)S(1)}, f32[192,2,768]{2,1,0:T(2,128)}, u32[]{:S(2)}) copy-start(f32[192,2,768]{2,1,0:T(2,128)} %param.14) | copy-start | bytes 3538948
  5.7 2.0 %copy-start.1 = (f32[3,128]{1,0:T(4,128)S(1)}, f32[3,128]{1,0:T(4,128)}, u32[]{:S(2)}) copy-start(f32[3,128]{1,0:T(4,128)} %param.9) | copy-start | bytes 4612
  5.7 2.0 %copy-start.2 = (f32[3,128]{1,0:T(4,128)S(1)}, f32[3,128]{1,0:T(4,128)}, u32[]{:S(2)}) copy-start(f32[3,128]{1,0:T(4,128)} %param.10) | copy-start | bytes 4612
